TPU v7x, 32 devices: a whole 2x2x4 slice. The times are simulated.
32 devices in a mesh: rep: 2 (over x), node: 2 (over core), ep: 8 (over z, y).
Axes of the slice: x: 2, y: 2, z: 4, core: 2. Of those that a mesh axis runs over, the one named last changes fastest.
Arguments:
- activations: bfloat16 [3072, 7168], P(('rep', 'node', 'ep')), parts along dimension 0, may hold values from -6 to 6
- expert_ids: int32 [3072, 8], P(('rep', 'node', 'ep')), parts along dimension 0, may hold values from 0 to 255, all different within a row; in each aligned block of 96 rows (0 to 95, 96 to 191, ...) at most 8 rows name the same one
- route_scores: float32 [3072, 8], P(('rep', 'node', 'ep')), parts along dimension 0, may hold values from 0.05 to 1
- capacity: int32 [256], replicated, may hold values from 6 to 8
- w_gate: bfloat16 [7168, 4096], P(None, ('node', 'ep')), may hold values from -0.0625 to 0.0625
- w_up: bfloat16 [7168, 4096], P(None, ('node', 'ep')), may hold values from -0.0625 to 0.0625
- w_down: bfloat16 [4096, 7168], P(('node', 'ep')), may hold values from -0.125 to 0.125
Outputs:
- mixed_out: bfloat16 [3072, 7168], P(('rep', 'node', 'ep')), parts along dimension 0
There are 2 independent parts, one for each index of `rep`. A program takes and returns all parts, laid end to end along the dimension named above; an argument that names none is the same for every part. Nothing has to cross between parts.
Inputs may be any that keep to these rules, and one draw needn't show every extreme that they name: `expert_ids`: each row names 8 different experts. In each aligned block of 96 rows (the rows of one device) no expert is named by more than 8 rows, and in some block one expert is named by exactly 8 rows.
All inputs are finite; a program needn't handle non-finite values.
Results may differ from a plain program's by a relative error of at most 0.007.
Values may be sent and summed in bfloat16 or wider, within the bound.
No kernel may reach another device: no remote copies, remote signals or barrier semaphores. Data moves between devices by JAX's collectives and lax.ppermute only.
A program may use at most 128 MiB of HBM per device.

v0:
```python
import jax
import jax.numpy as jnp
from jax import lax
from jax.sharding import PartitionSpec as P

TOPK = 8
SHARDS = 8
SEND_CAP = 8


def shards(activations, expert_ids, route_scores, capacity, w_gate, w_up, w_down):
    n_node = lax.axis_size("node")
    n_ep = lax.axis_size("ep")
    window = n_node * (n_ep // SHARDS)
    tok_rows = activations.shape[0]
    model_width = activations.shape[1]
    send_cap = SEND_CAP
    route_weight = (2.5 * route_scores / jnp.sum(route_scores, axis=1, keepdims=True)).astype(
        jnp.bfloat16
    )
    flat_ids = expert_ids.reshape(-1)
    expert_iota = jnp.arange(window, dtype=jnp.int32)
    onehot = (flat_ids[:, None] == expert_iota[None, :]).astype(jnp.int32)
    running = jnp.cumsum(onehot, axis=0)
    ranking = jnp.sum(onehot * running, axis=1) - 1
    limits = jnp.sum(onehot * capacity[:window][None, :], axis=1)
    is_live = (flat_ids < window) & (ranking < limits)
    slot_index = jnp.where(is_live, ranking * window + flat_ids, -1).reshape(tok_rows, TOPK)
    positions = jnp.arange(send_cap * window, dtype=jnp.int32)
    matches = slot_index[:, :, None] == positions[None, None, :]
    select = jnp.any(matches, axis=1).astype(jnp.bfloat16)
    combine_w = jnp.sum(
        jnp.where(matches, route_weight[:, :, None].astype(jnp.float32), 0.0), axis=1
    ).astype(jnp.bfloat16)
    expert_rows = lax.dot_general(
        select, activations, (((0,), (0,)), ((), ())), preferred_element_type=jnp.float32
    ).astype(jnp.bfloat16)
    copies = jnp.broadcast_to(
        expert_rows.reshape(send_cap, window, 1, model_width),
        (send_cap, window, SHARDS, model_width),
    )
    copies = copies.reshape(send_cap, window * SHARDS * model_width)
    received = lax.all_to_all(copies, ("node", "ep"), split_axis=1, concat_axis=0, tiled=True)
    gate_act = jnp.dot(received, w_gate, preferred_element_type=jnp.float32)
    up_act = jnp.dot(received, w_up, preferred_element_type=jnp.float32)
    inner_act = (jax.nn.silu(gate_act) * up_act).astype(jnp.bfloat16)
    partial_value = jnp.dot(inner_act, w_down, preferred_element_type=jnp.float32).astype(
        jnp.bfloat16
    )
    returned = lax.all_to_all(
        partial_value, ("node", "ep"), split_axis=0, concat_axis=1, tiled=True
    )
    summed = jnp.sum(
        returned.reshape(send_cap, window, SHARDS, model_width).astype(jnp.float32), axis=2
    )
    expert_out = summed.astype(jnp.bfloat16).reshape(send_cap * window, model_width)
    mixed_out = jnp.dot(combine_w, expert_out, preferred_element_type=jnp.float32)
    return mixed_out.astype(jnp.bfloat16)


def solution(mesh):
    placed = (
        P(("rep", "node", "ep"), None),
        P(("rep", "node", "ep"), None),
        P(("rep", "node", "ep"), None),
        P(),
        P(None, ("node", "ep")),
        P(None, ("node", "ep")),
        P(("node", "ep"), None),
    )
    return jax.shard_map(
        shards,
        mesh=mesh,
        in_specs=placed,
        out_specs=P(("rep", "node", "ep"), None),
        check_vma=False,
    )
```

profile of v0, /device:TPU:0, one launch (start us, length us, event | category | flops | bytes accessed | tf_op | source)
XLA Modules:
  0.0 111.7 jit_solution(11825912123103637743)
XLA Ops:
  0.0 0.0 copy-start
  0.0 0.9 copy.40
  0.9 0.1 eq.42
  1.0 0.1 eq.38
  1.1 0.7 slice.11
  1.8 0.6 reduce-window.6
  2.3 0.2 slice_reduce_fusion
  2.5 0.2 reduce-window.9
  2.7 0.1 add_bitcast_fusion
  2.8 0.1 select_reduce_fusion.1
  2.9 0.1 lt.15
  3.0 0.1 copy.42
  3.1 0.1 mul.36
  3.2 0.1 copy.43
  3.3 0.7 add_select_fusion
  4.0 0.0 copy-done
  4.0 0.3 convolution_convert_fusion.2
  4.3 0.1 broadcast_in_dim.28
  4.4 0.2 broadcast_in_dim.29
  4.6 0.0 copy-start.1
  4.6 51.5 %all_to_all.35 = bf16[8,16,7168]{2,0,1:T(8,128)(2,1)S(1)} all-to-all(bf16[8,16,7168]{2,0,1:T(8,128)(2,1)S(1)} %bitcast.42), channel_id=1, replica_groups=mesh['rep'=2,'node'=2,'ep'=8] {'node','ep'}, dimensions={1} | all-to-all | bytes 3670016 | tf_op jit(solution)/shard_map/all_to_all | solution.py:43
  56.1 0.0 copy-done.1
  56.2 0.7 fusion.3
  56.8 6.5 %fusion = bf16[16,8,7168]{2,1,0:T(8,128)(2,1)} fusion(bf16[256,7168]{1,0:T(8,128)(2,1)} %param.13, bf16[7168,256]{1,0:T(8,128)(2,1)} %param.12, bf16[8,16,7168]{2,0,1:T(8,128)(2,1)S(1)} %all_to_all.35, f32[128,256]{1,0:T(8,128)S(1)} %fusion.3), kind=kOutput, calls=%fused_computation.2 | convolution fusion | flops 940638208 | bytes 11141120 | tf_op jit(solution)/shard_map/dot_general | solution.py:47
  63.4 0.0 copy-start.2
  63.4 3.8 %all-to-all-start.1 = ((bf16[16,8,7168]{2,1,0:T(8,128)(2,1)}), bf16[16,8,7168]{2,1,0:T(8,128)(2,1)S(1)}, u32[]{:S(2)}, u32[]{:S(2)}) async-start(bf16[16,8,7168]{2,1,0:T(8,128)(2,1)} %fusion), calls=%async_computation.1 | async-start | bytes 3670016 | tf_op jit(solution)/shard_map/all_to_all | solution.py:50
  67.2 0.0 copy-done.2
  67.3 42.2 %all-to-all-done.1 = bf16[16,8,7168]{2,1,0:T(8,128)(2,1)S(1)} async-done(((bf16[16,8,7168]{2,1,0:T(8,128)(2,1)}), bf16[16,8,7168]{2,1,0:T(8,128)(2,1)S(1)}, u32[]{:S(2)}, u32[]{:S(2)}) %all-to-all-start.1) | async-done | bytes 1835040 | tf_op jit(solution)/shard_map/all_to_all | solution.py:50
  109.5 0.2 bitcast_reduce_fusion
  109.8 0.2 copy.45
  110.0 0.1 reshape.59
  110.1 1.6 %convolution_convert_fusion.1 = bf16[96,7168]{1,0:T(8,128)(2,1)} fusion(bf16[16,7168]{1,0:T(8,128)(2,1)S(1)} %reshape.59, bf16[96,16]{0,1:T(8,128)(2,1)S(1)} %select_reduce_fusion), kind=kOutput, calls=%fused_computation.1 | convolution fusion | flops 22708224 | bytes 1608704 | tf_op jit(solution)/shard_map/dot_general | solution.py:57
  (8 shorter events, 0.1 us)
Async XLA Ops:
  0.0 4.0 %copy-start = (bf16[96,7168]{1,0:T(8,128)(2,1)S(1)}, bf16[96,7168]{1,0:T(8,128)(2,1)}, u32[]{:S(2)}) copy-start(bf16[96,7168]{1,0:T(8,128)(2,1)} %param.7) | copy-start | bytes 4128772
  4.6 51.5 %copy-start.1 = (bf16[7168,256]{1,0:T(8,128)(2,1)S(1)}, bf16[7168,256]{1,0:T(8,128)(2,1)}, u32[]{:S(2)}) copy-start(bf16[7168,256]{1,0:T(8,128)(2,1)} %param.11) | copy-start | bytes 11010052
  63.4 3.9 %copy-start.2 = (f32[96,8]{0,1:T(8,128)S(1)}, f32[96,8]{0,1:T(8,128)}, u32[]{:S(2)}) copy-start(f32[96,8]{0,1:T(8,128)} %param.9) | copy-start | bytes 9220
  63.4 46.1 %all-to-all-start.1 = ((bf16[16,8,7168]{2,1,0:T(8,128)(2,1)}), bf16[16,8,7168]{2,1,0:T(8,128)(2,1)S(1)}, u32[]{:S(2)}, u32[]{:S(2)}) async-start(bf16[16,8,7168]{2,1,0:T(8,128)(2,1)} %fusion), calls=%async_computation.1 | async-start | bytes 3670016 | tf_op jit(solution)/shard_map/all_to_all | solution.py:50
where the time goes:
time: 112 us
  blocking collectives  51.5 us (46%)
  waiting for transfers between devices  42.2 us (38%)
  matrix products  9.13 us (8%)
  starting transfers between devices  3.84 us (3%)
  local copies, waits for them, and re-layouts  2.92 us (3%)
  other arithmetic  1.94 us (2%)
    all_to_all x1, blocking collectives, shards(): lax.all_to_all(copies, ('node', 'ep'), split_axis=1, concat_axis=0, tiled...  51.5 us
    all_to_all x1, waiting for transfers between devices, shards(): lax.all_to_all(partial_value, ('node', 'ep'), split_axis=0, concat_axis=1...  42.2 us
    dot_general x1, matrix products, shards(): jnp.dot(inner_act, w_down, preferred_element_type=jnp.float32)  6.55 us
    all_to_all x1, starting transfers between devices, shards(): lax.all_to_all(partial_value, ('node', 'ep'), split_axis=0, concat_axis=1...  3.84 us
  transfers between devices with their start and end apart: 1, of which 1 were waited for; matrix products, arithmetic and copies ran while one was open for 0% of the time, Pallas kernels for 0%

commit v1 on v0

--- a/solution.py
+++ b/solution.py
@@ -9,6 +9,14 @@
 
 
 def shards(activations, expert_ids, route_scores, capacity, w_gate, w_up, w_down):
+
+    def perform_copies(x0):
+        u1 = lax.axis_size(("node", "ep"))
+        carry_out = jnp.split(x0, u1, 0)
+        field_out = jnp.stack(carry_out, 0)
+        known = lax.all_to_all(field_out, ("node", "ep"), 0, 0)
+        return jnp.concatenate(known, 1)
+
     n_node = lax.axis_size("node")
     n_ep = lax.axis_size("ep")
     window = n_node * (n_ep // SHARDS)
@@ -47,9 +55,7 @@
     partial_value = jnp.dot(inner_act, w_down, preferred_element_type=jnp.float32).astype(
         jnp.bfloat16
     )
-    returned = lax.all_to_all(
-        partial_value, ("node", "ep"), split_axis=0, concat_axis=1, tiled=True
-    )
+    returned = perform_copies(partial_value)
     summed = jnp.sum(
         returned.reshape(send_cap, window, SHARDS, model_width).astype(jnp.float32), axis=2
     )

time: 112 us -> 137 us (1.22)
  local copies, waits for them, and re-layouts: 2.92 us -> 27.7 us
    unnamed x7 -> x22, local copies, waits for them, and re-layouts: 0.9 us -> 24.2 us
    another operation x0 -> x1, local copies, waits for them, and re-layouts: none -> 1.55 us  [perform_copies(): field_out = jnp.stack(carry_out, 0)]
where the time goes in v1:
time: 137 us
  blocking collectives  51.5 us (38%)
  waiting for transfers between devices  42.2 us (31%)
  local copies, waits for them, and re-layouts  27.7 us (20%)
  matrix products  9.13 us (7%)
  starting transfers between devices  3.84 us (3%)
  other arithmetic  1.94 us (1%)
    all_to_all x1, blocking collectives, shards(): lax.all_to_all(copies, ('node', 'ep'), split_axis=1, concat_axis=0, tiled...  51.5 us
    all_to_all x1, waiting for transfers between devices, perform_copies(): known = lax.all_to_all(field_out, ('node', 'ep'), 0, 0)  42.2 us
    unnamed x22, local copies, waits for them, and re-layouts  24.2 us
    dot_general x1, matrix products, shards(): jnp.dot(inner_act, w_down, preferred_element_type=jnp.float32)  6.55 us
    all_to_all x1, starting transfers between devices, perform_copies(): known = lax.all_to_all(field_out, ('node', 'ep'), 0, 0)  3.84 us
  transfers between devices with their start and end apart: 1, of which 1 were waited for; matrix products, arithmetic and copies ran while one was open for 0% of the time, Pallas kernels for 0%

profile of v1, /device:TPU:0, one launch (start us, length us, event | category | flops | bytes accessed | tf_op | source)
XLA Modules:
  0.0 136.5 jit_solution(17642227425404167115)
XLA Ops:
  0.0 0.9 copy.40
  1.1 0.7 slice.11
  1.8 0.6 reduce-window.6
  2.3 0.2 slice_reduce_fusion
  2.5 0.2 reduce-window.9
  3.3 0.7 add_select_fusion
  4.0 0.3 convolution_convert_fusion.2
  4.4 0.2 broadcast_in_dim.29
  4.6 51.5 %all_to_all.24 = bf16[8,16,7168]{2,0,1:T(8,128)(2,1)S(1)} all-to-all(bf16[8,16,7168]{2,0,1:T(8,128)(2,1)S(1)} %bitcast.104), channel_id=1, replica_groups=mesh['rep'=2,'node'=2,'ep'=8] {'node','ep'}, dimensions={1} | all-to-all | bytes 3670016 | tf_op jit(solution)/shard_map/all_to_all | solution.py:51
  56.2 0.7 fusion.2
  56.8 6.5 %convolution_convert_fusion = bf16[128,7168]{1,0:T(8,128)(2,1)} fusion(bf16[256,7168]{1,0:T(8,128)(2,1)} %param.13, bf16[7168,256]{1,0:T(8,128)(2,1)} %param.12, bf16[8,16,7168]{2,0,1:T(8,128)(2,1)S(1)} %all_to_all.24, f32[128,256]{1,0:T(8,128)S(1)} %fusion.2), kind=kOutput, calls=%fused_computation | convolution fusion | flops 940638208 | bytes 11141120 | tf_op jit(solution)/shard_map/dot_general | solution.py:55
  63.4 1.5 %fusion.32 = bf16[16,8,7168]{2,1,0:T(8,128)(2,1)} fusion(bf16[128,7168]{1,0:T(8,128)(2,1)} %convolution_convert_fusion), kind=kLoop, calls=%fused_computation.46 | loop fusion | bytes 229376
  64.9 1.6 %fusion.31 = bf16[16,8,7168]{2,1,0:T(8,128)(2,1)} fusion(bf16[16,8,7168]{2,1,0:T(8,128)(2,1)} %fusion.32, bf16[128,7168]{1,0:T(8,128)(2,1)} %convolution_convert_fusion), kind=kLoop, calls=%fused_computation.44 | loop fusion | bytes 229376
  66.5 1.6 %fusion.30 = bf16[16,8,7168]{2,1,0:T(8,128)(2,1)} fusion(bf16[16,8,7168]{2,1,0:T(8,128)(2,1)} %fusion.31, bf16[128,7168]{1,0:T(8,128)(2,1)} %convolution_convert_fusion), kind=kLoop, calls=%fused_computation.42 | loop fusion | bytes 229376
  68.0 1.5 %fusion.29 = bf16[16,8,7168]{2,1,0:T(8,128)(2,1)} fusion(bf16[16,8,7168]{2,1,0:T(8,128)(2,1)} %fusion.30, bf16[128,7168]{1,0:T(8,128)(2,1)} %convolution_convert_fusion), kind=kLoop, calls=%fused_computation.40 | loop fusion | bytes 229376
  69.6 1.5 %fusion.28 = bf16[16,8,7168]{2,1,0:T(8,128)(2,1)} fusion(bf16[16,8,7168]{2,1,0:T(8,128)(2,1)} %fusion.29, bf16[128,7168]{1,0:T(8,128)(2,1)} %convolution_convert_fusion), kind=kLoop, calls=%fused_computation.38 | loop fusion | bytes 229376
  71.1 1.5 %fusion.27 = bf16[16,8,7168]{2,1,0:T(8,128)(2,1)} fusion(bf16[16,8,7168]{2,1,0:T(8,128)(2,1)} %fusion.28, bf16[128,7168]{1,0:T(8,128)(2,1)} %convolution_convert_fusion), kind=kLoop, calls=%fused_computation.36 | loop fusion | bytes 229376
  72.7 1.6 %fusion.26 = bf16[16,8,7168]{2,1,0:T(8,128)(2,1)} fusion(bf16[16,8,7168]{2,1,0:T(8,128)(2,1)} %fusion.27, bf16[128,7168]{1,0:T(8,128)(2,1)} %convolution_convert_fusion), kind=kLoop, calls=%fused_computation.34 | loop fusion | bytes 229376
  74.2 1.5 %fusion.25 = bf16[16,8,7168]{2,1,0:T(8,128)(2,1)} fusion(bf16[16,8,7168]{2,1,0:T(8,128)(2,1)} %fusion.26, bf16[128,7168]{1,0:T(8,128)(2,1)} %convolution_convert_fusion), kind=kLoop, calls=%fused_computation.32 | loop fusion | bytes 229376
  75.8 1.6 %fusion.24 = bf16[16,8,7168]{2,1,0:T(8,128)(2,1)} fusion(bf16[16,8,7168]{2,1,0:T(8,128)(2,1)} %fusion.25, bf16[128,7168]{1,0:T(8,128)(2,1)} %convolution_convert_fusion), kind=kLoop, calls=%fused_computation.30 | loop fusion | bytes 229376
  77.3 1.5 %fusion.23 = bf16[16,8,7168]{2,1,0:T(8,128)(2,1)} fusion(bf16[16,8,7168]{2,1,0:T(8,128)(2,1)} %fusion.24, bf16[128,7168]{1,0:T(8,128)(2,1)} %convolution_convert_fusion), kind=kLoop, calls=%fused_computation.28 | loop fusion | bytes 229376
  78.9 1.6 %fusion.22 = bf16[16,8,7168]{2,1,0:T(8,128)(2,1)} fusion(bf16[16,8,7168]{2,1,0:T(8,128)(2,1)} %fusion.23, bf16[128,7168]{1,0:T(8,128)(2,1)} %convolution_convert_fusion), kind=kLoop, calls=%fused_computation.26 | loop fusion | bytes 229376
  80.4 1.6 %fusion.21 = bf16[16,8,7168]{2,1,0:T(8,128)(2,1)} fusion(bf16[16,8,7168]{2,1,0:T(8,128)(2,1)} %fusion.22, bf16[128,7168]{1,0:T(8,128)(2,1)} %convolution_convert_fusion), kind=kLoop, calls=%fused_computation.24 | loop fusion | bytes 229376
  82.0 1.5 %fusion.20 = bf16[16,8,7168]{2,1,0:T(8,128)(2,1)} fusion(bf16[16,8,7168]{2,1,0:T(8,128)(2,1)} %fusion.21, bf16[128,7168]{1,0:T(8,128)(2,1)} %convolution_convert_fusion), kind=kLoop, calls=%fused_computation.22 | loop fusion | bytes 229376
  83.5 1.6 %fusion.19 = bf16[16,8,7168]{2,1,0:T(8,128)(2,1)} fusion(bf16[16,8,7168]{2,1,0:T(8,128)(2,1)} %fusion.20, bf16[128,7168]{1,0:T(8,128)(2,1)} %convolution_convert_fusion), kind=kLoop, calls=%fused_computation.20 | loop fusion | bytes 229376
  85.1 1.6 %fusion.18 = bf16[16,8,7168]{2,1,0:T(8,128)(2,1)} fusion(bf16[16,8,7168]{2,1,0:T(8,128)(2,1)} %fusion.19, bf16[128,7168]{1,0:T(8,128)(2,1)} %convolution_convert_fusion), kind=kLoop, calls=%fused_computation.18 | loop fusion | bytes 229376
  86.7 1.5 %fusion.17 = bf16[16,8,7168]{2,1,0:T(8,128)(2,1)} fusion(bf16[16,8,7168]{2,1,0:T(8,128)(2,1)} %fusion.18, bf16[128,7168]{1,0:T(8,128)(2,1)} %convolution_convert_fusion), kind=kLoop, calls=%fused_computation.16 | loop fusion | bytes 229376 | tf_op jit(solution)/shard_map/stack | solution.py:16
  88.2 3.8 %all-to-all-start.1 = ((bf16[16,8,7168]{2,1,0:T(8,128)(2,1)}), bf16[16,8,7168]{2,1,0:T(8,128)(2,1)S(1)}, u32[]{:S(2)}, u32[]{:S(2)}) async-start(bf16[16,8,7168]{2,1,0:T(8,128)(2,1)} %fusion.17), calls=%async_computation.1 | async-start | bytes 3670016 | tf_op jit(solution)/shard_map/all_to_all | solution.py:17
  92.1 42.2 %all-to-all-done.1 = bf16[16,8,7168]{2,1,0:T(8,128)(2,1)S(1)} async-done(((bf16[16,8,7168]{2,1,0:T(8,128)(2,1)}), bf16[16,8,7168]{2,1,0:T(8,128)(2,1)S(1)}, u32[]{:S(2)}, u32[]{:S(2)}) %all-to-all-start.1) | async-done | bytes 1835040 | tf_op jit(solution)/shard_map/all_to_all | solution.py:17
  134.3 0.2 bitcast_reduce_fusion
  134.6 0.2 copy.45
  134.9 1.6 %convolution_convert_fusion.1 = bf16[96,7168]{1,0:T(8,128)(2,1)} fusion(bf16[16,7168]{1,0:T(8,128)(2,1)S(1)} %reshape.55, bf16[96,16]{0,1:T(8,128)(2,1)S(1)} %select_reduce_fusion), kind=kOutput, calls=%fused_computation.1 | convolution fusion | flops 22708224 | bytes 1608704 | tf_op jit(solution)/shard_map/dot_general | solution.py:63
  (24 shorter events, 1.0 us)
Async XLA Ops:
  0.0 4.0 %copy-start = (bf16[96,7168]{1,0:T(8,128)(2,1)S(1)}, bf16[96,7168]{1,0:T(8,128)(2,1)}, u32[]{:S(2)}) copy-start(bf16[96,7168]{1,0:T(8,128)(2,1)} %param.7) | copy-start | bytes 4128772
  4.6 51.5 %copy-start.1 = (bf16[7168,256]{1,0:T(8,128)(2,1)S(1)}, bf16[7168,256]{1,0:T(8,128)(2,1)}, u32[]{:S(2)}) copy-start(bf16[7168,256]{1,0:T(8,128)(2,1)} %param.11) | copy-start | bytes 11010052
  88.2 3.9 %copy-start.2 = (f32[96,8]{0,1:T(8,128)S(1)}, f32[96,8]{0,1:T(8,128)}, u32[]{:S(2)}) copy-start(f32[96,8]{0,1:T(8,128)} %param.9) | copy-start | bytes 9220
  88.2 46.1 %all-to-all-start.1 = ((bf16[16,8,7168]{2,1,0:T(8,128)(2,1)}), bf16[16,8,7168]{2,1,0:T(8,128)(2,1)S(1)}, u32[]{:S(2)}, u32[]{:S(2)}) async-start(bf16[16,8,7168]{2,1,0:T(8,128)(2,1)} %fusion.17), calls=%async_computation.1 | async-start | bytes 3670016 | tf_op jit(solution)/shard_map/all_to_all | solution.py:17
